TPU v7x, 32 devices: a whole 2x2x4 slice. The times are simulated.
32 devices in a mesh: shard: 8 (over y, x, core), rep: 4 (over z).
Axes of the slice: x: 2, y: 2, z: 4, core: 2. Of those that a mesh axis runs over, the one named last changes fastest.
Arguments:
- tokens: bfloat16 [4, 1024, 1600], P('rep', 'shard'), may hold values from -6 to 6
- segment_ids: int32 [4, 1024], P('rep'), may hold values from 0 to 3, never falling along the last dimension, each value on 1 to 512 neighbouring positions
- ln1_gain: bfloat16 [1600], P('shard'), may hold values from 0.5 to 1.5
- ln1_bias: bfloat16 [1600], P('shard'), may hold values from -2.5 to 2.5
- w_qkv: bfloat16 [1600, 4800], P('shard')
- q_bias: bfloat16 [1600], P('shard'), may hold values from -2.5 to 2.5
- v_bias: bfloat16 [1600], P('shard'), may hold values from -2.5 to 2.5
- w_out: bfloat16 [1600, 1600], P('shard'), may hold values from -0.625 to 0.625
- out_bias: bfloat16 [1600], P('shard'), may hold values from -2.5 to 2.5
- ln2_gain: bfloat16 [1600], P('shard'), may hold values from 0.5 to 1.5
- ln2_bias: bfloat16 [1600], P('shard'), may hold values from -2.5 to 2.5
- w_fc: bfloat16 [1600, 6400], P('shard'), may hold values from -0.15625 to 0.15625
- fc_bias: bfloat16 [6400], P('shard'), may hold values from -2.5 to 2.5
- w_proj: bfloat16 [6400, 1600], P('shard'), may hold values from -0.078125 to 0.078125
- proj_bias: bfloat16 [1600], P('shard'), may hold values from -2.5 to 2.5
- grad_out: bfloat16 [4, 1024, 1600], P('rep', 'shard'), may hold values from -6 to 6
Outputs:
- output: float32 [4, 1024, 1600], P('rep', 'shard')
- grad_tokens: float32 [4, 1024, 1600], P('rep', 'shard')
- grad_ln1_gain: float32 [1600], P('shard')
- grad_ln1_bias: float32 [1600], P('shard')
- grad_w_qkv: float32 [1600, 4800], P('shard', 'rep')
- grad_q_bias: float32 [1600], P('shard')
- grad_v_bias: float32 [1600], P('shard')
- grad_w_out: float32 [1600, 1600], P('shard', 'rep')
- grad_out_bias: float32 [1600], P('shard')
- grad_ln2_gain: float32 [1600], P('shard')
- grad_ln2_bias: float32 [1600], P('shard')
- grad_w_fc: float32 [1600, 6400], P('shard', 'rep')
- grad_fc_bias: float32 [6400], P('shard')
- grad_w_proj: float32 [6400, 1600], P('shard', 'rep')
- grad_proj_bias: float32 [1600], P('shard')
Inputs may be any that keep to these rules, and one draw needn't show every extreme that they name: `segment_ids`: along each sequence the document numbers never fall, and one document covers at most 512 positions.
All inputs are finite; a program needn't handle non-finite values.
Results may differ from a plain program's by a relative error of at most 0.019.
Values may be sent and summed in bfloat16 or wider, within the bound.
No kernel may reach another device: no remote copies, remote signals or barrier semaphores. Data moves between devices by JAX's collectives and lax.ppermute only.
A program may use at most 576 MiB of HBM per device.

v0:
```python
import math
import jax
import jax.numpy as jnp
from jax import lax
from jax.sharding import PartitionSpec as P

HD = 64
EPSILON = 1e-05
GELU_SCALE = math.sqrt(2.0 / math.pi)


def layer_norm(values, gain, shift):
    centre_val = jnp.mean(values, axis=-1, keepdims=True)
    centred = values - centre_val
    variance = jnp.mean(centred * centred, axis=-1, keepdims=True)
    inverse = lax.rsqrt(variance + EPSILON)
    normed = centred * inverse
    return (normed * gain + shift, normed, inverse)


def norm_back(upstream, normed, inverse, gain):
    scaled = upstream * gain
    return inverse * (
        scaled
        - jnp.mean(scaled, axis=-1, keepdims=True)
        - normed * jnp.mean(scaled * normed, axis=-1, keepdims=True)
    )


def gelu_value(inputs_pre):
    cubic = inputs_pre * inputs_pre * inputs_pre
    return 0.5 * inputs_pre * (1.0 + jnp.tanh(GELU_SCALE * (inputs_pre + 0.044715 * cubic)))


def gelu_slope(inputs_pre):
    square = inputs_pre * inputs_pre
    tangent = jnp.tanh(GELU_SCALE * (inputs_pre + 0.044715 * square * inputs_pre))
    return 0.5 * (1.0 + tangent) + 0.5 * inputs_pre * (1.0 - tangent * tangent) * GELU_SCALE * (
        1.0 + 3.0 * 0.044715 * square
    )


def score_table(queries, keys, key_mask, score_scale):
    scores = (
        jnp.einsum("sqhe,skhe->shqk", queries, keys, preferred_element_type=jnp.float32)
        * score_scale
    )
    return jnp.where(key_mask[:, None], scores, -1e30)


def attend(queries, keys, values, key_mask, score_scale):
    scores = score_table(queries, keys, key_mask, score_scale)
    row_max = jnp.max(scores, axis=-1, keepdims=True)
    log_total = row_max + jnp.log(jnp.sum(jnp.exp(scores - row_max), axis=-1, keepdims=True))
    weights_soft = jnp.where(key_mask[:, None], jnp.exp(scores - log_total), 0.0).astype(
        jnp.bfloat16
    )
    mixed = jnp.einsum("shqk,skhe->sqhe", weights_soft, values, preferred_element_type=jnp.float32)
    return (mixed, log_total)


def attend_back(queries, keys, values, key_mask, log_total, grad_mixed, score_scale):
    scores = score_table(queries, keys, key_mask, score_scale)
    weights_soft = jnp.where(key_mask[:, None], jnp.exp(scores - log_total), 0.0)
    grad_soft = jnp.einsum(
        "sqhe,skhe->shqk", grad_mixed, values, preferred_element_type=jnp.float32
    )
    delta = jnp.sum(weights_soft * grad_soft, axis=-1, keepdims=True)
    grad_scores = (weights_soft * (grad_soft - delta) * score_scale).astype(jnp.bfloat16)
    grad_q = jnp.einsum("shqk,skhe->sqhe", grad_scores, keys, preferred_element_type=jnp.float32)
    grad_k = jnp.einsum("shqk,sqhe->skhe", grad_scores, queries, preferred_element_type=jnp.float32)
    grad_v = jnp.einsum(
        "shqk,sqhe->skhe",
        weights_soft.astype(jnp.bfloat16),
        grad_mixed,
        preferred_element_type=jnp.float32,
    )
    return (grad_q, grad_k, grad_v)


def add_rows(operand, shard_rows):
    return jnp.dot(operand, shard_rows, preferred_element_type=jnp.float32)


def back_rows(operand, shard_rows):
    return lax.dot_general(
        operand, shard_rows, (((1,), (1,)), ((), ())), preferred_element_type=jnp.float32
    )


def cross_rows(operand, other):
    return lax.dot_general(
        operand, other, (((0,), (0,)), ((), ())), preferred_element_type=jnp.float32
    )


def local(
    tokens,
    segment_ids,
    ln1_gain,
    ln1_bias,
    w_qkv,
    q_bias,
    v_bias,
    w_out,
    out_bias,
    ln2_gain,
    ln2_bias,
    w_fc,
    fc_bias,
    w_proj,
    proj_bias,
    grad_out,
):
    seq_count, local_len, model_width = tokens.shape
    full_len = segment_ids.shape[1]
    row_count = seq_count * local_len
    head_count = model_width // HD
    score_scale = float(HD) ** (-0.5)
    own_rows = ln1_gain.shape[0]
    hidden_width = w_fc.shape[1]
    fc_ratio = hidden_width // model_width
    own_hidden = own_rows * fc_ratio
    small = (
        lax.all_gather(ln1_gain, "shard", axis=0, tiled=True),
        lax.all_gather(ln1_bias, "shard", axis=0, tiled=True),
        lax.all_gather(q_bias, "shard", axis=0, tiled=True),
        lax.all_gather(v_bias, "shard", axis=0, tiled=True),
        lax.all_gather(out_bias, "shard", axis=0, tiled=True),
        lax.all_gather(ln2_gain, "shard", axis=0, tiled=True),
        lax.all_gather(ln2_bias, "shard", axis=0, tiled=True),
        lax.all_gather(fc_bias, "shard", axis=0, tiled=True),
        lax.all_gather(proj_bias, "shard", axis=0, tiled=True),
    )
    gain_one, shift_one, bias_q, bias_v, bias_out, gain_two, shift_two, bias_fc, bias_proj = [
        member.astype(jnp.float32) for member in small
    ]
    first_pos = lax.axis_index("shard") * local_len
    query_pos = first_pos + jnp.arange(local_len, dtype=jnp.int32)
    key_pos = jnp.arange(full_len, dtype=jnp.int32)
    query_seg = lax.dynamic_slice_in_dim(segment_ids, first_pos, local_len, 1)
    key_mask = (key_pos[None, None, :] <= query_pos[None, :, None]) & (
        query_seg[:, :, None] == segment_ids[:, None, :]
    )
    resid_in = tokens.reshape(row_count, model_width).astype(jnp.float32)
    ln_one, normed_one, inverse_one = layer_norm(resid_in, gain_one, shift_one)
    ln_one_b = ln_one.astype(jnp.bfloat16)
    qkv = add_rows(ln_one_b, lax.all_gather(w_qkv, "shard", axis=0, tiled=True))
    queries = (
        (qkv[:, :model_width] + bias_q)
        .astype(jnp.bfloat16)
        .reshape(seq_count, local_len, head_count, HD)
    )
    key_local = (
        qkv[:, model_width : 2 * model_width]
        .astype(jnp.bfloat16)
        .reshape(seq_count, local_len, model_width)
    )
    value_local = (
        (qkv[:, 2 * model_width :] + bias_v)
        .astype(jnp.bfloat16)
        .reshape(seq_count, local_len, model_width)
    )
    keys_all, values_all = (
        lax.all_gather(key_local, "shard", axis=1, tiled=True),
        lax.all_gather(value_local, "shard", axis=1, tiled=True),
    )
    keys = keys_all.reshape(seq_count, full_len, head_count, HD)
    values = values_all.reshape(seq_count, full_len, head_count, HD)

    def attend_one(items):
        one_q, one_k, one_v, one_mask = items
        one_mixed, one_total = attend(
            one_q[None], one_k[None], one_v[None], one_mask[None], score_scale
        )
        return (one_mixed[0], one_total[0])

    mixed, log_total = lax.map(attend_one, (queries, keys, values, key_mask))
    attended = mixed.reshape(row_count, model_width).astype(jnp.bfloat16)
    attn_proj = add_rows(attended, lax.all_gather(w_out, "shard", axis=0, tiled=True))
    mid = resid_in + attn_proj + bias_out
    ln_two, normed_two, inverse_two = layer_norm(mid, gain_two, shift_two)
    ln_two_b = ln_two.astype(jnp.bfloat16)
    fc_whole, proj_whole = (
        lax.all_gather(w_fc, "shard", axis=0, tiled=True),
        lax.all_gather(w_proj, "shard", axis=0, tiled=True),
    )
    pre_act = jnp.dot(ln_two_b, fc_whole, preferred_element_type=jnp.float32) + bias_fc
    hidden = gelu_value(pre_act).astype(jnp.bfloat16)
    result = mid + jnp.dot(hidden, proj_whole, preferred_element_type=jnp.float32) + bias_proj
    grad_round = grad_out.reshape(row_count, model_width)
    grad_top = grad_round.astype(jnp.float32)
    back_proj, back_fc = (
        lax.all_gather(w_proj, "shard", axis=0, tiled=True),
        lax.all_gather(w_fc, "shard", axis=0, tiled=True),
    )
    grad_hidden = back_rows(grad_round, back_proj)
    grad_pre = grad_hidden * gelu_slope(pre_act)
    grad_pre_round = grad_pre.astype(jnp.bfloat16)
    grad_ln_two = back_rows(grad_pre_round, back_fc)
    grad_mid = grad_top + norm_back(grad_ln_two, normed_two, inverse_two, gain_two)
    grad_mid_round = grad_mid.astype(jnp.bfloat16)
    back_out, back_qkv = (
        lax.all_gather(w_out, "shard", axis=0, tiled=True),
        lax.all_gather(w_qkv, "shard", axis=0, tiled=True),
    )
    grad_attn = back_rows(grad_mid_round, back_out)
    grad_attended = grad_attn.astype(jnp.bfloat16).reshape(seq_count, local_len, head_count, HD)

    def attend_one_back(items):
        one_q, one_k, one_v, one_mask, one_total, one_grad = items
        part_q, part_k, part_v = attend_back(
            one_q[None],
            one_k[None],
            one_v[None],
            one_mask[None],
            one_total[None],
            one_grad[None],
            score_scale,
        )
        return (part_q[0], part_k[0], part_v[0])

    grad_q, grad_k_all, grad_v_all = lax.map(
        attend_one_back, (queries, keys, values, key_mask, log_total, grad_attended)
    )
    grad_k_own, grad_v_own = (
        lax.psum_scatter(
            grad_k_all.reshape(seq_count, full_len, model_width).astype(jnp.bfloat16),
            "shard",
            scatter_dimension=1,
            tiled=True,
        ).astype(jnp.float32),
        lax.psum_scatter(
            grad_v_all.reshape(seq_count, full_len, model_width).astype(jnp.bfloat16),
            "shard",
            scatter_dimension=1,
            tiled=True,
        ).astype(jnp.float32),
    )
    grad_q = grad_q.reshape(row_count, model_width)
    grad_k_own = grad_k_own.reshape(row_count, model_width)
    grad_v_own = grad_v_own.reshape(row_count, model_width)
    grad_qkv = jnp.concatenate([grad_q, grad_k_own, grad_v_own], axis=1).astype(jnp.bfloat16)
    grad_ln_one = back_rows(grad_qkv, back_qkv)
    grad_in = grad_mid + norm_back(grad_ln_one, normed_one, inverse_one, gain_one)
    small_cols = jnp.concatenate(
        [
            jnp.stack(
                [
                    jnp.sum(grad_ln_one * normed_one, axis=0),
                    jnp.sum(grad_ln_one, axis=0),
                    jnp.sum(grad_q, axis=0),
                    jnp.sum(grad_v_own, axis=0),
                    jnp.sum(grad_mid, axis=0),
                    jnp.sum(grad_ln_two * normed_two, axis=0),
                    jnp.sum(grad_ln_two, axis=0),
                    jnp.sum(grad_top, axis=0),
                ],
                axis=1,
            ),
            jnp.sum(grad_pre, axis=0).reshape(model_width, fc_ratio),
            jnp.zeros((model_width, 128 - 8 - fc_ratio), jnp.float32),
        ],
        axis=1,
    )
    part_qkv = cross_rows(ln_one_b, grad_qkv)
    part_out = cross_rows(attended, grad_mid_round)
    part_fc = cross_rows(ln_two_b, grad_pre_round)
    part_proj = cross_rows(hidden, grad_round).reshape(
        own_rows * lax.axis_size("shard"), fc_ratio * model_width
    )
    owned = lax.psum_scatter(
        jnp.concatenate([part_qkv, part_out, part_fc, part_proj, small_cols], axis=1).astype(
            jnp.bfloat16
        ),
        "shard",
        scatter_dimension=0,
        tiled=True,
    ).astype(jnp.float32)
    base = 4 * model_width + hidden_width + fc_ratio * model_width
    parts = (
        owned[:, : 3 * model_width],
        owned[:, 3 * model_width : 4 * model_width],
        owned[:, 4 * model_width : 4 * model_width + hidden_width],
        owned[:, 4 * model_width + hidden_width : base].reshape(own_hidden, model_width),
    )
    small_own = owned[:, base:]
    total_qkv, total_out, total_fc, total_proj = (
        lax.psum_scatter(
            parts[0].astype(jnp.bfloat16), "rep", scatter_dimension=1, tiled=True
        ).astype(jnp.float32),
        lax.psum_scatter(
            parts[1].astype(jnp.bfloat16), "rep", scatter_dimension=1, tiled=True
        ).astype(jnp.float32),
        lax.psum_scatter(
            parts[2].astype(jnp.bfloat16), "rep", scatter_dimension=1, tiled=True
        ).astype(jnp.float32),
        lax.psum_scatter(
            parts[3].astype(jnp.bfloat16), "rep", scatter_dimension=1, tiled=True
        ).astype(jnp.float32),
    )
    total_small = lax.psum(small_own.astype(jnp.bfloat16), "rep").astype(jnp.float32)
    return (
        result.reshape(seq_count, local_len, model_width),
        grad_in.reshape(seq_count, local_len, model_width),
        total_small[:, 0],
        total_small[:, 1],
        total_qkv,
        total_small[:, 2],
        total_small[:, 3],
        total_out,
        total_small[:, 4],
        total_small[:, 5],
        total_small[:, 6],
        total_fc,
        total_small[:, 8 : 8 + fc_ratio].reshape(own_hidden),
        total_proj,
        total_small[:, 7],
    )


def solution(mesh):
    return jax.shard_map(
        local,
        mesh=mesh,
        in_specs=(
            P("rep", "shard", None),
            P("rep", None),
            P("shard"),
            P("shard"),
            P("shard", None),
            P("shard"),
            P("shard"),
            P("shard", None),
            P("shard"),
            P("shard"),
            P("shard"),
            P("shard", None),
            P("shard"),
            P("shard", None),
            P("shard"),
            P("rep", "shard", None),
        ),
        out_specs=(
            P("rep", "shard", None),
            P("rep", "shard", None),
            P("shard"),
            P("shard"),
            P("shard", "rep"),
            P("shard"),
            P("shard"),
            P("shard", "rep"),
            P("shard"),
            P("shard"),
            P("shard"),
            P("shard", "rep"),
            P("shard"),
            P("shard", "rep"),
            P("shard"),
        ),
        check_vma=False,
    )
```

profile of v0, /device:TPU:0, one launch (start us, length us, event | category | flops | bytes accessed | tf_op | source)
XLA Modules:
  0.0 1772.5 jit_solution(15159649565087665562)
XLA Ops:
  18.3 29.0 %all-reduce.10 = (bf16[1600]{0:T(1024)(128)(2,1)S(1)}, bf16[1600]{0:T(1024)(128)(2,1)S(1)}, bf16[1600]{0:T(1024)(128)(2,1)S(1)}, bf16[1600]{0:T(1024)(128)(2,1)S...) all-reduce(bf16[1600]{0:T(1024)(128)(2,1)S(1)} %dynamic-update-slic, ...), channel_id=1, replica_groups=mesh['shard'=8,'rep'=4] {'shard'}, use_global_device_ids=true, to_apply=%add.1 | all-reduce | flops 19200 | bytes 76800
  49.7 48.3 %all-gather.9.cloned.1.call-done = bf16[1600,4800]{1,0:T(8,128)(2,1)} async-done(((bf16[200,4800]{1,0:T(8,128)(2,1)}), bf16[1600,4800]{1,0:T(8,128)(2,1)}) %all-gather.9.cloned.1.call-update) | async-done | bytes 15360016 | tf_op jit(solution)/shard_map/all_gather | solution.py:148
  113.0 29.8 %all-gather.19.cloned.1.call-done = bf16[1024,1600]{0,1:T(8,128)(2,1)} async-done(((bf16[128,1600]{0,1:T(8,128)(2,1)}), bf16[1024,1600]{0,1:T(8,128)(2,1)}) %all-gather.19.cloned.1.call-update) | async-done | bytes 3276816 | tf_op jit(solution)/shard_map/all_gather | solution.py:165
  151.8 26.8 %all-gather.17.cloned.1.call-done = bf16[1024,1600]{0,1:T(8,128)(2,1)} async-done(((bf16[128,1600]{0,1:T(8,128)(2,1)}), bf16[1024,1600]{0,1:T(8,128)(2,1)}) %all-gather.17.cloned.1.call-update) | async-done | bytes 3276816 | tf_op jit(solution)/shard_map/all_gather | solution.py:166
  187.0 34.7 %all-gather.11.cloned.1.call-done = bf16[1600,1600]{1,0:T(8,128)(2,1)} async-done(((bf16[200,1600]{1,0:T(8,128)(2,1)}), bf16[1600,1600]{1,0:T(8,128)(2,1)}) %all-gather.11.cloned.1.call-update) | async-done | bytes 5120016 | tf_op jit(solution)/shard_map/all_gather | solution.py:180
  226.8 102.1 %all-gather.13.cloned.1.call-done = bf16[1600,6400]{1,0:T(8,128)(2,1)} async-done(((bf16[200,6400]{1,0:T(8,128)(2,1)}), bf16[1600,6400]{1,0:T(8,128)(2,1)}) %all-gather.13.cloned.1.call-update) | async-done | bytes 20480016 | tf_op jit(solution)/shard_map/all_gather | solution.py:185
  328.8 12.4 convolution_add_fusion
  341.2 98.2 %all-gather.15.cloned.1.call-done = bf16[6400,1600]{1,0:T(8,128)(2,1)} async-done(((bf16[800,1600]{1,0:T(8,128)(2,1)}), bf16[6400,1600]{1,0:T(8,128)(2,1)}) %all-gather.15.cloned.1.call-update) | async-done | bytes 20480016 | tf_op jit(solution)/shard_map/all_gather | solution.py:186
  439.5 12.4 fusion.99
  451.9 12.1 multiply_reduce_fusion.1
  473.5 16.2 copy.55
  505.2 33.4 %fusion.40 = bf16[25,64,1024]{2,1,0:T(8,128)(2,1)} fusion(bf16[128,25,64]{0,2,1:T(8,128)(2,1)S(1)} %bitcast.144, f32[25,128,1024]{2,1,0:T(8,128)} %fusion.100, f32[25,128,1024]{2,1,0:T(8,128)} %copy-done, f32[25,128]{1,0:T(8,128)S(1)} %log_add_fusion, pred[128,1024]{1,0:T(8,128)(4,1)S(1)} %fusion.69), kind=kOutput, calls=%fused_computation.48 | convolution fusion | flops 450564224 | bytes 30044672 | tf_op jit(solution)/shard_map/while/body/eval_jaxpr/shqk,sqhe->skhe/dot_general | solution.py:71
  538.6 16.3 copy.53
  561.6 12.7 convolution_convert_fusion
  574.3 30.6 %copy.43 = bf16[6400,1600]{1,0:T(8,128)(2,1)} copy(bf16[6400,1600]{0,1:T(8,128)(2,1)} %convolution_convert_fusion) | data formatting | bytes 40960000 | tf_op jit(solution)/shard_map/convert.29
  605.0 35.8 %reshape.340 = bf16[1600,6400]{1,0:T(8,128)(2,1)} reshape(bf16[6400,1600]{1,0:T(8,128)(2,1)} %copy.43) | data formatting | bytes 40960000 | tf_op jit(solution)/shard_map/reshape | solution.py:269
  640.8 33.8 %fusion.93 = (bf16[25,64]{1,0:T(8,128)(2,1)S(1)}, bf16[1,128,25,64]{1,3,2,0:T(8,128)(2,1)}) fusion(bf16[1024,25,64]{0,2,1:T(8,128)(2,1)} %bitcast.138, f32[25,128,1024]{2,1,0:T(8,128)} %fusion.100, f32[25,128,1024]{2,1,0:T(8,128)} %copy-done, f32[25,128]{1,0:T(8,128)S(1)} %log_add_fusion, pred[128,1024]{1,0:T(8,128)(4,1)S(1)} %fusion.69), kind=kOutput, calls=%fused_computation.128 | convolution fusion | flops 449333824 | bytes 30047872 | tf_op jit(solution)/shard_map/while/body/eval_jaxpr/shqk,skhe->sqhe/dot_general | solution.py:70
  714.8 10.9 fusion.62
  729.6 130.5 %concatenate.9 = bf16[1600,19328]{1,0:T(8,128)(2,1)} concatenate(bf16[1600,4800]{1,0:T(8,128)(2,1)} %convolution_convert_fusion.2, bf16[1600,1600]{1,0:T(8,128)(2,1)} %convolution_convert_fusion.3, bf16[1600,6400]{1,0:T(8,128)(2,1)} %convolution_convert_fusion.1, bf16[1600,6400]{1,0:T(8,128)(2,1)} %reshape.340, bf16[1600,1]{1,0:T(8,128)(2,1)} %stack.40, bf16[1600,1]{1,0:T(8,128)(2,1)} %stack.41, ...), dimensions={1} | concatenate | bytes 123699200 | tf_op jit(solution)/shard_map/concatenate | solution.py:273
  860.9 699.7 %all-reduce.13.cloned.1.call-done = bf16[1600,19328]{1,0:T(8,128)(2,1)} async-done(((bf16[1600,19328]{1,0:T(8,128)(2,1)}), bf16[1600,19328]{1,0:T(8,128)(2,1)}) %all-reduce.13.cloned.1.call-update) | async-done | bytes 61849616
  1593.5 15.0 fusion.39
  1611.8 22.2 %psum.7 = bf16[200,128]{1,0:T(8,128)(2,1)S(1)} all-reduce(bf16[200,128]{1,0:T(8,128)(2,1)S(1)} %dynamic-slice.11), channel_id=1, replica_groups=mesh['shard'=8,'rep'=4] {'rep'}, use_global_device_ids=true, to_apply=%region_23.24 | all-reduce | flops 25600 | bytes 102400 | tf_op jit(solution)/shard_map/psum | solution.py:302
  1642.8 61.9 %reduce-scatter.27.cloned.1.call-done = bf16[1600,200]{1,0:T(8,128)(2,1)} async-done(((bf16[6400,200]{1,0:T(8,128)(2,1)}), bf16[1600,200]{1,0:T(8,128)(2,1)}) %reduce-scatter.27.cloned.1.call-update) | async-done | bytes 640016
  1707.3 55.9 %reduce-scatter.17.cloned.1.call-done = bf16[800,400]{0,1:T(8,128)(2,1)} async-done(((bf16[800,1600]{0,1:T(8,128)(2,1)}), bf16[800,400]{0,1:T(8,128)(2,1)}) %reduce-scatter.17.cloned.1.call-update) | async-done | bytes 640016 | tf_op jit(solution)/shard_map/reduce_scatter | solution.py:298
  (165 shorter events, 175.0 us)
Async XLA Ops:
  7.2 90.9 %all-gather.9.cloned.1.call-start = ((), (), s32[]{:S(2)}) async-start(), calls=%async_computation.6 | async-start | bytes 17510400 | tf_op jit(solution)/shard_map/all_gather | solution.py:148
  7.9 134.9 %all-gather.19.cloned.1.call-start = ((), (), s32[]{:S(2)}) async-start(), calls=%async_computation.12 | async-start | bytes 3686400 | tf_op jit(solution)/shard_map/all_gather | solution.py:165
  109.4 69.2 %all-gather.17.cloned.1.call-start = ((), (), s32[]{:S(2)}) async-start(), calls=%async_computation.11 | async-start | bytes 3686400 | tf_op jit(solution)/shard_map/all_gather | solution.py:166
  110.7 36.5 %copy-start.11 = (bf16[128,1600]{0,1:T(8,128)(2,1)}, bf16[128,1600]{0,1:T(8,128)(2,1)S(1)}, u32[]{:S(2)}) copy-start(bf16[128,1600]{0,1:T(8,128)(2,1)S(1)} %get-tuple-element.97) | copy-start | bytes 1228804
  110.7 111.0 %all-gather.11.cloned.1.call-start = ((), (), s32[]{:S(2)}) async-start(), calls=%async_computation.7 | async-start | bytes 5990400 | tf_op jit(solution)/shard_map/all_gather | solution.py:180
  111.3 217.6 %all-gather.13.cloned.1.call-start = ((), (), s32[]{:S(2)}) async-start(), calls=%async_computation.8 | async-start | bytes 23040000 | tf_op jit(solution)/shard_map/all_gather | solution.py:185
  111.8 327.6 %all-gather.15.cloned.1.call-start = ((), (), s32[]{:S(2)}) async-start(), calls=%async_computation.9 | async-start | bytes 23961600 | tf_op jit(solution)/shard_map/all_gather | solution.py:186
  112.4 582.1 %reduce-scatter.21.cloned.1.call-start = ((), (), s32[]{:S(2)}) async-start(), calls=%async_computation.14 | async-start | bytes 3833856
  178.6 43.1 %copy-start.1 = (bf16[1,128,1600]{1,2,0:T(8,128)(2,1)S(1)}, bf16[1,128,1600]{1,2,0:T(8,128)(2,1)}, u32[]{:S(2)}) copy-start(bf16[1,128,1600]{1,2,0:T(8,128)(2,1)} %param.16) | copy-start | bytes 1228804
  186.9 39.6 %copy-start.8 = (bf16[25,64,128]{2,1,0:T(8,128)(2,1)}, bf16[25,64,128]{2,1,0:T(8,128)(2,1)S(1)}, u32[]{:S(2)}) copy-start(bf16[25,64,128]{2,1,0:T(8,128)(2,1)S(1)} %convolution_convert_fusion.6) | copy-start | bytes 1228804
  226.8 212.7 %copy-start.5 = (bf16[1,128,1600]{1,2,0:T(8,128)(2,1)S(1)}, bf16[1,128,1600]{1,2,0:T(8,128)(2,1)}, u32[]{:S(2)}) copy-start(bf16[1,128,1600]{1,2,0:T(8,128)(2,1)} %param.31) | copy-start | bytes 1228804
  439.5 29.5 %slice-start = ((s8[13107200]{0:T(1024)(128)(4,1)}), s8[4194304]{0:T(1024)(128)(4,1)S(1)}, s32[]{:S(2)}) async-start(s8[13107200]{0:T(1024)(128)(4,1)} %bitcast.124), calls=%async_computation.19 | async-start | bytes 8388608
  439.5 29.5 %slice-start.1 = ((s8[13107200]{0:T(1024)(128)(4,1)}), s8[524288]{0:T(1024)(128)(4,1)S(1)}, s32[]{:S(2)}) async-start(s8[13107200]{0:T(1024)(128)(4,1)} %bitcast.124), calls=%async_computation.20 | async-start | bytes 1048576
  451.9 17.1 slice-start.2
  451.9 17.1 slice-start.3
  495.1 205.0 %reduce-scatter.19.cloned.1.call-start = ((), (), s32[]{:S(2)}) async-start(), calls=%async_computation.13 | async-start | bytes 3833856
  560.1 1000.5 %all-reduce.13.cloned.1.call-start = ((), (), s32[]{:S(2)}) async-start(), calls=%async_computation.18 | async-start | bytes 123699200
  640.8 39.4 %copy-start.3 = (f32[128,1600]{0,1:T(8,128)S(1)}, f32[128,1600]{0,1:T(8,128)}, u32[]{:S(2)}) copy-start(f32[128,1600]{0,1:T(8,128)} %copy-done.2) | copy-start | bytes 2457604
  640.8 39.4 %copy-start.9 = (bf16[25,64,128]{2,1,0:T(8,128)(2,1)S(1)}, bf16[25,64,128]{2,1,0:T(8,128)(2,1)}, u32[]{:S(2)}) copy-start(bf16[25,64,128]{2,1,0:T(8,128)(2,1)} %copy-done.8) | copy-start | bytes 1228804
  714.8 14.8 copy-start.10
  860.2 775.8 %reduce-scatter.25.cloned.1.call-start = ((), (), s32[]{:S(2)}) async-start(), calls=%async_computation.16 | async-start | bytes 1024000
  1563.2 77.3 %reduce-scatter.23.cloned.1.call-start = ((), (), s32[]{:S(2)}) async-start(), calls=%async_computation.15 | async-start | bytes 3072000
  1570.4 134.3 %reduce-scatter.27.cloned.1.call-start = ((), (), s32[]{:S(2)}) async-start(), calls=%async_computation.17 | async-start | bytes 4096000
  1582.4 180.9 %reduce-scatter.17.cloned.1.call-start = ((), (), s32[]{:S(2)}) async-start(), calls=%async_computation.10 | async-start | bytes 3584000 | tf_op jit(solution)/shard_map/reduce_scatter | solution.py:298
  (9 other events, 41.5 us)
Sparse Core Ops, SparseCore 0:
  9.9 88.1 all-gather.8
  109.5 33.2 all-gather.18
  145.3 33.2 all-gather.16
  180.3 41.3 all-gather.10
  223.4 105.3 all-gather.12
  330.6 108.8 all-gather.14
  495.2 47.4 reduce-scatter.20
  560.2 47.4 reduce-scatter.18
  860.3 700.2 all-reduce.12
  1563.3 23.7 reduce-scatter.24
  1589.4 50.9 reduce-scatter.22
  1642.6 62.0 reduce-scatter.26
  1707.0 56.2 reduce-scatter.16
where the time goes:
time: 1790 us; the launch traced here: 1770 us
  waiting for transfers between devices  1160 us (65%)
  local copies, waits for them, and re-layouts  311 us (17%)
  matrix products  213 us (12%)
  blocking collectives  51.2 us (3%)
    unnamed x19, waiting for transfers between devices  767 us
    concatenate x1, local copies, waits for them, and re-layouts, local(): jnp.concatenate([part_qkv, part_out, part_fc, part_proj, small_cols], axi...  131 us
    all_gather x1, waiting for transfers between devices, local(): lax.all_gather(w_fc, 'shard', axis=0, tiled=True)  102 us
    all_gather x1, waiting for transfers between devices, local(): lax.all_gather(w_proj, 'shard', axis=0, tiled=True)  98.2 us
    unnamed x72, local copies, waits for them, and re-layouts  76.8 us
    reduce_scatter x1, waiting for transfers between devices, local(): lax.psum_scatter(parts[3].astype(jnp.bfloat16), 'rep', scatter_dimension=...  55.9 us
    all_gather x1, waiting for transfers between devices, local(): qkv = add_rows(ln_one_b, lax.all_gather(w_qkv, 'shard', axis=0, tiled=True))  48.3 us
    dot_general x4, matrix products, back_rows(): lax.dot_general(operand, shard_rows, (((1,), (1,)), ((), ())), preferred_...  39.8 us
  transfers between devices with their start and end apart: 13, of which 10 were waited for; matrix products, arithmetic and copies ran while one was open for 17% of the time, Pallas kernels for 0%

commit v1 on v0

--- a/solution.py
+++ b/solution.py
@@ -7,6 +7,24 @@
 HD = 64
 EPSILON = 1e-05
 GELU_SCALE = math.sqrt(2.0 / math.pi)
+
+
+def ring_gather(shard, axis, dim):
+    ways, here, step = (lax.axis_size(axis), lax.axis_index(axis), shard.shape[dim])
+    dims = [n * ways if d == dim else n for d, n in enumerate(shard.shape)]
+    full = lax.dynamic_update_slice_in_dim(
+        jnp.zeros(dims, shard.dtype), shard, here * step, axis=dim
+    )
+    going_up = going_down = shard
+    for far in range(1, ways // 2 + 1):
+        going_up = lax.ppermute(going_up, axis, [(d, (d + 1) % ways) for d in range(ways)])
+        full = lax.dynamic_update_slice_in_dim(full, going_up, (here - far) % ways * step, axis=dim)
+        if 2 * far < ways:
+            going_down = lax.ppermute(going_down, axis, [(d, (d - 1) % ways) for d in range(ways)])
+            full = lax.dynamic_update_slice_in_dim(
+                full, going_down, (here + far) % ways * step, axis=dim
+            )
+    return full
 
 
 def layer_norm(values, gain, shift):
@@ -182,7 +200,7 @@
     ln_two, normed_two, inverse_two = layer_norm(mid, gain_two, shift_two)
     ln_two_b = ln_two.astype(jnp.bfloat16)
     fc_whole, proj_whole = (
-        lax.all_gather(w_fc, "shard", axis=0, tiled=True),
+        ring_gather(w_fc, "shard", 0),
         lax.all_gather(w_proj, "shard", axis=0, tiled=True),
     )
     pre_act = jnp.dot(ln_two_b, fc_whole, preferred_element_type=jnp.float32) + bias_fc

time: 1790 us -> 1890 us (1.056)
  waiting for transfers between devices: 1160 us -> 1210 us
  local copies, waits for them, and re-layouts: 311 us -> 335 us
    ppermute x0 -> x7, waiting for transfers between devices: none -> 299 us  [the longest x4 288 us: ring_gather(): lax.ppermute(going_up, axis, [(d, (d + 1) % ways) for d in range(ways)])]
    all_gather x1, waiting for transfers between devices: 98.2 us -> 0.01 us  [local(): lax.all_gather(w_proj, 'shard', axis=0, tiled=True)]
    all_gather x1, waiting for transfers between devices: 102 us -> 41.3 us  [local(): lax.all_gather(w_fc, 'shard', axis=0, tiled=True)]
    all_gather x1, waiting for transfers between devices: 34.7 us -> 0.02 us  [local(): lax.all_gather(w_out, 'shard', axis=0, tiled=True)]
    all_gather x1, waiting for transfers between devices: 29.8 us -> 0.01 us  [local(): lax.all_gather(key_local, 'shard', axis=1, tiled=True)]
    all_gather x1, waiting for transfers between devices: 26.8 us -> 0.02 us  [local(): lax.all_gather(value_local, 'shard', axis=1, tiled=True)]
    dynamic_update_slice x0 -> x8, local copies, waits for them, and re-layouts: none -> 19.7 us  [the longest x4 10.6 us: ring_gather(): lax.dynamic_update_slice_in_dim(full, going_up, (here - far) % ways * ste...]
    unnamed x72 -> x86, local copies, waits for them, and re-layouts: 76.8 us -> 73.5 us
  transfers between devices with their start and end apart: 13 -> 20, of which waited for: 10 -> 12; matrix products, arithmetic and copies ran while one was open for 17% -> 19% of each run, Pallas kernels for 0% -> 0%
where the time goes in v1:
time: 1890 us; the launch traced here: 1870 us
  waiting for transfers between devices  1210 us (64%)
  local copies, waits for them, and re-layouts  335 us (18%)
  matrix products  226 us (12%)
  blocking collectives  51.2 us (3%)
    unnamed x19, waiting for transfers between devices  768 us
    ppermute x4, waiting for transfers between devices, ring_gather(): lax.ppermute(going_up, axis, [(d, (d + 1) % ways) for d in range(ways)])  288 us
    concatenate x1, local copies, waits for them, and re-layouts, local(): jnp.concatenate([part_qkv, part_out, part_fc, part_proj, small_cols], axi...  130 us
    unnamed x86, local copies, waits for them, and re-layouts  73.5 us
    reduce_scatter x1, waiting for transfers between devices, local(): lax.psum_scatter(parts[3].astype(jnp.bfloat16), 'rep', scatter_dimension=...  55.9 us
    all_gather x1, waiting for transfers between devices, local(): qkv = add_rows(ln_one_b, lax.all_gather(w_qkv, 'shard', axis=0, tiled=True))  48.3 us
    all_gather x1, waiting for transfers between devices, local(): lax.all_gather(w_fc, 'shard', axis=0, tiled=True)  41.3 us
    dot_general x4, matrix products, back_rows(): lax.dot_general(operand, shard_rows, (((1,), (1,)), ((), ())), preferred_...  38 us
  transfers between devices with their start and end apart: 20, of which 12 were waited for; matrix products, arithmetic and copies ran while one was open for 19% of the time, Pallas kernels for 0%

profile of v1, /device:TPU:0, one launch (start us, length us, event | category | flops | bytes accessed | tf_op | source)
XLA Modules:
  0.0 1868.5 jit_solution(11149643619965822903)
XLA Ops:
  18.3 29.0 %all-reduce.10 = (bf16[1600]{0:T(1024)(128)(2,1)S(1)}, bf16[1600]{0:T(1024)(128)(2,1)S(1)}, bf16[1600]{0:T(1024)(128)(2,1)S(1)}, bf16[1600]{0:T(1024)(128)(2,1)S...) all-reduce(bf16[1600]{0:T(1024)(128)(2,1)S(1)} %dynamic-update-slic, ...), channel_id=1, replica_groups=mesh['shard'=8,'rep'=4] {'shard'}, use_global_device_ids=true, to_apply=%add.1 | all-reduce | flops 19200 | bytes 76800
  49.7 48.3 %all-gather.9.cloned.1.call-done = bf16[1600,4800]{1,0:T(8,128)(2,1)} async-done(((bf16[200,4800]{1,0:T(8,128)(2,1)}), bf16[1600,4800]{1,0:T(8,128)(2,1)}) %all-gather.9.cloned.1.call-update) | async-done | bytes 15360016 | tf_op jit(solution)/shard_map/all_gather | solution.py:166
  98.0 13.7 fusion.87
  121.0 76.8 %collective-permute-done = bf16[200,6400]{1,0:T(8,128)(2,1)} collective-permute-done((bf16[200,6400]{1,0:T(8,128)(2,1)S(1)}, bf16[200,6400]{1,0:T(8,128)(2,1)}, u32[]{:S(2)}, u32[]{:S(2)}) %collective-permute-start) | collective-permute-done | bytes 2560032 | tf_op jit(solution)/shard_map/ppermute | solution.py:20
  212.4 66.9 %collective-permute-done.2 = bf16[200,6400]{1,0:T(8,128)(2,1)} collective-permute-done((bf16[200,6400]{1,0:T(8,128)(2,1)}, bf16[200,6400]{1,0:T(8,128)(2,1)}, u32[]{:S(2)}, u32[]{:S(2)}) %collective-permute-start.2) | collective-permute-done | bytes 2560032 | tf_op jit(solution)/shard_map/ppermute | solution.py:20
  293.1 84.9 %collective-permute-done.4 = bf16[200,6400]{1,0:T(8,128)(2,1)S(1)} collective-permute-done((bf16[200,6400]{1,0:T(8,128)(2,1)}, bf16[200,6400]{1,0:T(8,128)(2,1)S(1)}, u32[]{:S(2)}, u32[]{:S(2)}) %collective-permute-start.4) | collective-permute-done | bytes 2560032 | tf_op jit(solution)/shard_map/ppermute | solution.py:20
  391.4 59.8 %collective-permute-done.6 = bf16[200,6400]{1,0:T(8,128)(2,1)S(1)} collective-permute-done((bf16[200,6400]{1,0:T(8,128)(2,1)S(1)}, bf16[200,6400]{1,0:T(8,128)(2,1)S(1)}, u32[]{:S(2)}, u32[]{:S(2)}) %collective-permute-start.6) | collective-permute-done | bytes 2560032 | tf_op jit(solution)/shard_map/ppermute | solution.py:20
  476.4 23.8 %convolution_add_fusion = f32[128,6400]{1,0:T(8,128)} fusion(bf16[1600,6400]{1,0:T(8,128)(2,1)} %constant_dynamic-update-slice_fusion, f32[6400]{0:T(1024)S(1)} %convert_element_type.174, f32[128,1600]{0,1:T(8,128)S(1)} %get-tuple-element.106, f32[1600]{0:T(1024)S(1)} %convert_element_type.172, f32[1600]{0:T(1024)S(1)} %convert_element_type.171, ...), kind=kOutput, calls=%fused_computation.11 | convolution fusion | flops 2623283200 | bytes 24615424 | tf_op jit(solution)/shard_map/dot_general | solution.py:206
  500.2 11.4 fusion.100
  511.6 41.3 %all-gather.15.cloned.1.call-done = bf16[1600,6400]{1,0:T(8,128)(2,1)} async-done(((bf16[200,6400]{1,0:T(8,128)(2,1)}), bf16[1600,6400]{1,0:T(8,128)(2,1)}) %all-gather.15.cloned.1.call-update) | async-done | bytes 20480016 | tf_op jit(solution)/shard_map/all_gather | solution.py:213
  552.9 11.7 multiply_reduce_fusion.1
  573.8 16.2 copy.55
  604.6 33.4 %fusion.40 = bf16[25,64,1024]{2,1,0:T(8,128)(2,1)} fusion(bf16[128,25,64]{0,2,1:T(8,128)(2,1)S(1)} %bitcast.144, f32[25,128,1024]{2,1,0:T(8,128)} %fusion.101, f32[25,128,1024]{2,1,0:T(8,128)} %copy-done, f32[25,128]{1,0:T(8,128)S(1)} %log_add_fusion, pred[128,1024]{1,0:T(8,128)(4,1)S(1)} %fusion.69), kind=kOutput, calls=%fused_computation.48 | convolution fusion | flops 450564224 | bytes 30044672 | tf_op jit(solution)/shard_map/while/body/eval_jaxpr/shqk,sqhe->skhe/dot_general | solution.py:89
  638.0 16.3 copy.53
  661.2 12.6 convolution_convert_fusion
  673.8 30.7 %copy.43 = bf16[6400,1600]{1,0:T(8,128)(2,1)} copy(bf16[6400,1600]{0,1:T(8,128)(2,1)} %convolution_convert_fusion) | data formatting | bytes 40960000 | tf_op jit(solution)/shard_map/convert.29
  704.5 35.8 %reshape.340 = bf16[1600,6400]{1,0:T(8,128)(2,1)} reshape(bf16[6400,1600]{1,0:T(8,128)(2,1)} %copy.43) | data formatting | bytes 40960000 | tf_op jit(solution)/shard_map/reshape | solution.py:287
  740.3 33.8 %fusion.94 = (bf16[25,64]{1,0:T(8,128)(2,1)S(1)}, bf16[1,128,25,64]{1,3,2,0:T(8,128)(2,1)}) fusion(bf16[1024,25,64]{0,2,1:T(8,128)(2,1)} %bitcast.138, f32[25,128,1024]{2,1,0:T(8,128)} %fusion.101, f32[25,128,1024]{2,1,0:T(8,128)} %copy-done, f32[25,128]{1,0:T(8,128)S(1)} %log_add_fusion, pred[128,1024]{1,0:T(8,128)(4,1)S(1)} %fusion.69), kind=kOutput, calls=%fused_computation.137 | convolution fusion | flops 449333824 | bytes 30047872 | tf_op jit(solution)/shard_map/while/body/eval_jaxpr/shqk,skhe->sqhe/dot_general | solution.py:88
  825.8 130.1 %concatenate.9 = bf16[1600,19328]{1,0:T(8,128)(2,1)} concatenate(bf16[1600,4800]{1,0:T(8,128)(2,1)} %convolution_convert_fusion.2, bf16[1600,1600]{1,0:T(8,128)(2,1)} %convolution_convert_fusion.3, bf16[1600,6400]{1,0:T(8,128)(2,1)} %convolution_convert_fusion.1, bf16[1600,6400]{1,0:T(8,128)(2,1)} %reshape.340, bf16[1600,1]{1,0:T(8,128)(2,1)} %stack.40, bf16[1600,1]{1,0:T(8,128)(2,1)} %stack.41, ...), dimensions={1} | concatenate | bytes 123699200 | tf_op jit(solution)/shard_map/concatenate | solution.py:291
  956.6 700.0 %all-reduce.13.cloned.1.call-done = bf16[1600,19328]{1,0:T(8,128)(2,1)} async-done(((bf16[1600,19328]{1,0:T(8,128)(2,1)}), bf16[1600,19328]{1,0:T(8,128)(2,1)}) %all-reduce.13.cloned.1.call-update) | async-done | bytes 61849616
  1689.8 15.0 fusion.39
  1707.0 22.3 %psum.7 = bf16[200,128]{1,0:T(8,128)(2,1)S(1)} all-reduce(bf16[200,128]{1,0:T(8,128)(2,1)S(1)} %dynamic-slice.11), channel_id=1, replica_groups=mesh['shard'=8,'rep'=4] {'rep'}, use_global_device_ids=true, to_apply=%region_23.24 | all-reduce | flops 25600 | bytes 102400 | tf_op jit(solution)/shard_map/psum | solution.py:320
  1739.0 61.7 %reduce-scatter.27.cloned.1.call-done = bf16[1600,200]{1,0:T(8,128)(2,1)} async-done(((bf16[6400,200]{1,0:T(8,128)(2,1)}), bf16[1600,200]{1,0:T(8,128)(2,1)}) %reduce-scatter.27.cloned.1.call-update) | async-done | bytes 640016
  1803.3 55.9 %reduce-scatter.17.cloned.1.call-done = bf16[800,400]{0,1:T(8,128)(2,1)} async-done(((bf16[800,1600]{0,1:T(8,128)(2,1)}), bf16[800,400]{0,1:T(8,128)(2,1)}) %reduce-scatter.17.cloned.1.call-update) | async-done | bytes 640016 | tf_op jit(solution)/shard_map/reduce_scatter | solution.py:316
  (202 shorter events, 220.5 us)
Async XLA Ops:
  7.2 90.9 %all-gather.9.cloned.1.call-start = ((), (), s32[]{:S(2)}) async-start(), calls=%async_computation.6 | async-start | bytes 17510400 | tf_op jit(solution)/shard_map/all_gather | solution.py:166
  7.9 444.9 %all-gather.19.cloned.1.call-start = ((), (), s32[]{:S(2)}) async-start(), calls=%async_computation.12 | async-start | bytes 3686400 | tf_op jit(solution)/shard_map/all_gather | solution.py:183
  47.2 50.8 %copy-start.15 = (f32[1600]{0:T(1024)}, f32[1600]{0:T(1024)S(1)}, u32[]{:S(2)}) copy-start(f32[1600]{0:T(1024)S(1)} %convert_element_type.159) | copy-start | bytes 19204
  111.7 86.3 %copy-start.21 = (s32[1,1024]{1,0:T(1,128)S(1)}, s32[1,1024]{1,0:T(1,128)}, u32[]{:S(2)}) copy-start(s32[1,1024]{1,0:T(1,128)} %param.17) | copy-start | bytes 12292
  113.8 349.1 %all-gather.17.cloned.1.call-start = ((), (), s32[]{:S(2)}) async-start(), calls=%async_computation.11 | async-start | bytes 3686400 | tf_op jit(solution)/shard_map/all_gather | solution.py:184
  116.5 336.3 %copy-start.10 = (bf16[128,1600]{0,1:T(8,128)(2,1)}, bf16[128,1600]{0,1:T(8,128)(2,1)S(1)}, u32[]{:S(2)}) copy-start(bf16[128,1600]{0,1:T(8,128)(2,1)S(1)} %get-tuple-element.97) | copy-start | bytes 1228804
  116.5 354.7 %all-gather.11.cloned.1.call-start = ((), (), s32[]{:S(2)}) async-start(), calls=%async_computation.7 | async-start | bytes 5990400 | tf_op jit(solution)/shard_map/all_gather | solution.py:198
  117.1 383.1 %all-gather.13.cloned.1.call-start = ((), (), s32[]{:S(2)}) async-start(), calls=%async_computation.8 | async-start | bytes 23961600 | tf_op jit(solution)/shard_map/all_gather | solution.py:204
  117.7 435.2 %all-gather.15.cloned.1.call-start = ((), (), s32[]{:S(2)}) async-start(), calls=%async_computation.9 | async-start | bytes 23040000 | tf_op jit(solution)/shard_map/all_gather | solution.py:213
  118.3 675.8 %reduce-scatter.21.cloned.1.call-start = ((), (), s32[]{:S(2)}) async-start(), calls=%async_computation.14 | async-start | bytes 3833856
  118.3 79.5 %collective-permute-start = (bf16[200,6400]{1,0:T(8,128)(2,1)S(1)}, bf16[200,6400]{1,0:T(8,128)(2,1)}, u32[]{:S(2)}, u32[]{:S(2)}) collective-permute-start(bf16[200,6400]{1,0:T(8,128)(2,1)S(1)} %copy-done.2), channel_id=1, source_target_pairs={{0,4},{4,8},{8,12},{12,16},{16,20},{20,24},{24,28},{28,0},{1,5},{5... | collective-permute-start | bytes 7680008 | tf_op jit(solution)/shard_map/ppermute | solution.py:20
  118.6 82.2 %collective-permute-start.1 = (bf16[200,6400]{1,0:T(8,128)(2,1)S(1)}, bf16[200,6400]{1,0:T(8,128)(2,1)}, u32[]{:S(2)}, u32[]{:S(2)}) collective-permute-start(bf16[200,6400]{1,0:T(8,128)(2,1)S(1)} %copy-done.2), channel_id=1, source_target_pairs={{0,28},{4,0},{8,4},{12,8},{16,12},{20,16},{24,20},{28,24},{1,29},{... | collective-permute-start | bytes 7680008 | tf_op jit(solution)/shard_map/ppermute | solution.py:23
  197.9 81.3 %collective-permute-start.2 = (bf16[200,6400]{1,0:T(8,128)(2,1)}, bf16[200,6400]{1,0:T(8,128)(2,1)}, u32[]{:S(2)}, u32[]{:S(2)}) collective-permute-start(bf16[200,6400]{1,0:T(8,128)(2,1)} %collective-permute-done), channel_id=1, source_target_pairs={{0,4},{4,8},{8,12},{12,16},{16,20},{20,24},{24,28},{28,0},{1,5},{5... | collective-permute-start | bytes 7680008 | tf_op jit(solution)/shard_map/ppermute | solution.py:20
  200.8 86.3 %collective-permute-start.3 = (bf16[200,6400]{1,0:T(8,128)(2,1)}, bf16[200,6400]{1,0:T(8,128)(2,1)S(1)}, u32[]{:S(2)}, u32[]{:S(2)}) collective-permute-start(bf16[200,6400]{1,0:T(8,128)(2,1)} %collective-permute-done.1), channel_id=1, source_target_pairs={{0,28},{4,0},{8,4},{12,8},{16,12},{20,16},{24,20},{28,24},{1,29},{... | collective-permute-start | bytes 7680008 | tf_op jit(solution)/shard_map/ppermute | solution.py:23
  279.2 98.8 %collective-permute-start.4 = (bf16[200,6400]{1,0:T(8,128)(2,1)}, bf16[200,6400]{1,0:T(8,128)(2,1)S(1)}, u32[]{:S(2)}, u32[]{:S(2)}) collective-permute-start(bf16[200,6400]{1,0:T(8,128)(2,1)} %collective-permute-done.2), channel_id=1, source_target_pairs={{0,4},{4,8},{8,12},{12,16},{16,20},{20,24},{24,28},{28,0},{1,5},{5... | collective-permute-start | bytes 7680008 | tf_op jit(solution)/shard_map/ppermute | solution.py:20
  287.1 102.5 %collective-permute-start.5 = (bf16[200,6400]{1,0:T(8,128)(2,1)S(1)}, bf16[200,6400]{1,0:T(8,128)(2,1)S(1)}, u32[]{:S(2)}, u32[]{:S(2)}) collective-permute-start(bf16[200,6400]{1,0:T(8,128)(2,1)S(1)} %collective-permute-done.3), channel_id=1, source_target_pairs={{0,28},{4,0},{8,4},{12,8},{16,12},{20,16},{24,20},{28,24},{1,29},{... | collective-permute-start | bytes 7680008 | tf_op jit(solution)/shard_map/ppermute | solution.py:23
  378.1 73.1 %collective-permute-start.6 = (bf16[200,6400]{1,0:T(8,128)(2,1)S(1)}, bf16[200,6400]{1,0:T(8,128)(2,1)S(1)}, u32[]{:S(2)}, u32[]{:S(2)}) collective-permute-start(bf16[200,6400]{1,0:T(8,128)(2,1)S(1)} %collective-permute-done.4), channel_id=1, source_target_pairs={{0,4},{4,8},{8,12},{12,16},{16,20},{20,24},{24,28},{28,0},{1,5},{5... | collective-permute-start | bytes 7680008 | tf_op jit(solution)/shard_map/ppermute | solution.py:20
  511.6 53.0 %copy-start.3 = (bf16[128,6400]{1,0:T(8,128)(2,1)}, bf16[128,6400]{1,0:T(8,128)(2,1)S(1)}, u32[]{:S(2)}) copy-start(bf16[128,6400]{1,0:T(8,128)(2,1)S(1)} %get-tuple-element.111) | copy-start | bytes 4915204
  595.3 202.6 %reduce-scatter.19.cloned.1.call-start = ((), (), s32[]{:S(2)}) async-start(), calls=%async_computation.13 | async-start | bytes 3833856
  659.4 997.2 %all-reduce.13.cloned.1.call-start = ((), (), s32[]{:S(2)}) async-start(), calls=%async_computation.18 | async-start | bytes 123699200
  955.9 775.3 %reduce-scatter.25.cloned.1.call-start = ((), (), s32[]{:S(2)}) async-start(), calls=%async_computation.16 | async-start | bytes 1024000
  1659.3 77.4 %reduce-scatter.23.cloned.1.call-start = ((), (), s32[]{:S(2)}) async-start(), calls=%async_computation.15 | async-start | bytes 3072000
  1666.4 134.3 %reduce-scatter.27.cloned.1.call-start = ((), (), s32[]{:S(2)}) async-start(), calls=%async_computation.17 | async-start | bytes 4096000
  1678.4 180.8 %reduce-scatter.17.cloned.1.call-start = ((), (), s32[]{:S(2)}) async-start(), calls=%async_computation.10 | async-start | bytes 3584000 | tf_op jit(solution)/shard_map/reduce_scatter | solution.py:316
  (23 other events, 459.8 us)
Sparse Core Ops, SparseCore 0:
  9.9 88.1 all-gather.8
  113.9 45.9 all-gather.18
  162.3 43.3 all-gather.16
  207.5 62.7 all-gather.10
  272.1 172.7 all-gather.12
  446.6 106.2 all-gather.14
  595.4 47.4 reduce-scatter.20
  659.6 47.2 reduce-scatter.18
  956.0 700.5 all-reduce.12
  1659.4 23.7 reduce-scatter.24
  1685.5 51.1 reduce-scatter.22
  1738.8 61.8 reduce-scatter.26
  1803.0 56.2 reduce-scatter.16
